TPU v7x, 32 devices: a whole 2x2x4 slice. The times are simulated.
32 devices in a mesh: dp: 8 (over z, x), tensor: 4 (over y, core).
Axes of the slice: x: 2, y: 2, z: 4, core: 2. Of those that a mesh axis runs over, the one named last changes fastest.
Arguments:
- inputs: bfloat16 [2048, 8192], P('dp', 'tensor'), may hold values from -6 to 6
- out_grads: bfloat16 [2048, 8192], P('dp', 'tensor'), may hold values from -6 to 6
- gate_pre: bfloat16 [2048, 28672], P('dp', 'tensor'), may hold values from -6 to 6
- up_pre: bfloat16 [2048, 28672], P('dp', 'tensor'), may hold values from -6 to 6
- hidden_grad: bfloat16 [2048, 28672], P('dp', 'tensor'), may hold values from -6 to 6
- proj_model: bfloat16 [8192, 128], P(('tensor', 'dp')), may hold values from -0.0625 to 0.0625
- proj_hidden: bfloat16 [28672, 192], P(('tensor', 'dp')), may hold values from -0.03125 to 0.03125
- lengths: int32 [8, 4], P('dp'), may hold values from 1 to 192, 256 in all within a row
- owners: int32 [8, 4], P('dp'), may hold values from 0 to 3, each once within a row
Outputs:
- features: float32 [32, 12288], P(('dp', 'tensor'))
Inputs may be any that keep to these rules, and one draw needn't show every extreme that they name: `lengths`: each row sums to 256, and each row has an example of exactly 192 tokens. `owners`: each row names every slot once.
All inputs are finite; a program needn't handle non-finite values.
Results may differ from a plain program's by a relative error of at most 0.0029.
Values may be sent and summed in bfloat16 or wider, within the bound.
A program may use at most 64 MiB of HBM per device.

v0:
```python
import jax
import jax.numpy as jnp
from jax import lax
from jax.sharding import PartitionSpec as P


def per_device(
    inputs, out_grads, gate_pre, up_pre, hidden_grad, proj_model, proj_hidden, lengths, owners
):
    rank_width = proj_model.shape[1] // 2
    tok_rows = inputs.shape[0]
    gate_value = gate_pre.astype(jnp.float32)
    up_value = up_pre.astype(jnp.float32)
    grad_value = hidden_grad.astype(jnp.float32)
    sigmoid_gate = jax.nn.sigmoid(gate_value)
    hidden = (gate_value * sigmoid_gate * up_value).astype(jnp.bfloat16)
    up_grad = (grad_value * gate_value * sigmoid_gate).astype(jnp.bfloat16)
    gate_grad = (
        grad_value * up_value * sigmoid_gate * (1.0 + gate_value * (1.0 - sigmoid_gate))
    ).astype(jnp.bfloat16)
    sources = (gate_grad, up_grad, hidden)
    block_rows = lax.all_gather(proj_hidden, "dp", axis=0, tiled=True)
    parts = []
    for column, source in enumerate(sources):
        parts.append(
            jnp.dot(
                source,
                block_rows[:, column * rank_width : (column + 1) * rank_width],
                preferred_element_type=jnp.float32,
            )
        )
    hidden_part = jnp.concatenate(parts, axis=1)
    block_rows = lax.all_gather(proj_model, "dp", axis=0, tiled=True)
    first_part = jnp.dot(inputs, block_rows[:, :rank_width], preferred_element_type=jnp.float32)
    second_part = jnp.dot(out_grads, block_rows[:, rank_width:], preferred_element_type=jnp.float32)
    model_part = jnp.concatenate([first_part, second_part], axis=1)
    partial_value = jnp.concatenate([hidden_part, model_part], axis=1)
    lens = lengths[0]
    owner_row = owners[0]
    starts = jnp.cumsum(lens) - lens
    myself = lax.axis_index("tensor")
    tensor_count = lax.axis_size("tensor")
    chosen = (owner_row == myself).astype(jnp.int32)
    my_length = jnp.sum(lens * chosen)
    capacity = 3 * tok_rows // tensor_count
    slots = jnp.arange(capacity * lax.axis_size("tensor"), dtype=jnp.int32)
    holder = slots // capacity
    within = slots % capacity
    matched = (owner_row[None, :] == holder[:, None]).astype(jnp.int32)
    first_token = jnp.sum(matched * starts[None, :], axis=1)
    span = jnp.sum(matched * lens[None, :], axis=1)
    valid = within < span
    picked = jnp.where(valid, first_token + within, 0)
    summed = lax.psum_scatter(
        jnp.take(partial_value, picked, axis=0) * valid[:, None].astype(jnp.float32),
        "tensor",
        scatter_dimension=0,
        tiled=True,
    )
    weights = (jnp.arange(capacity, dtype=jnp.int32) < my_length).astype(jnp.float32)

    def block_of(index):
        return summed[:, index * rank_width : (index + 1) * rank_width]

    pairs = ((0, 3), (1, 3), (4, 2))
    blocks = []
    for left_index, right_index in pairs:
        left_side = block_of(left_index) * weights[:, None]
        blocks.append(
            jnp.einsum(
                "ta,tb->ab", left_side, block_of(right_index), precision=lax.Precision.HIGHEST
            )
        )
    return jnp.stack(blocks, axis=0).reshape(1, 3 * rank_width * rank_width)


def solution(mesh):
    in_specs = (
        P("dp", "tensor"),
        P("dp", "tensor"),
        P("dp", "tensor"),
        P("dp", "tensor"),
        P("dp", "tensor"),
        P(("tensor", "dp"), None),
        P(("tensor", "dp"), None),
        P("dp", None),
        P("dp", None),
    )
    out_specs = P(("dp", "tensor"), None)
    return jax.shard_map(
        per_device, mesh=mesh, in_specs=in_specs, out_specs=out_specs, check_vma=False
    )
```

profile of v0, /device:TPU:0, one launch (start us, length us, event | category | flops | bytes accessed | tf_op | source)
XLA Modules:
  0.0 123.5 jit_solution(9361023392948454162)
XLA Ops:
  6.5 0.0 copy-start
  6.5 0.0 all-gather.2.cloned.1.call-start
  6.5 0.7 all-gather.2.cloned.1.call-update
  7.3 0.0 reduce-scatter.2.cloned.1.call-start
  7.3 0.8 reduce-window_clone.1
  8.1 0.7 subtract_bitcast_fusion
  8.8 0.8 fusion.36
  9.6 34.1 %all_gather.7 = bf16[2048,128]{1,0:T(8,128)(2,1)S(1)} all-gather(bf16[256,128]{1,0:T(8,128)(2,1)} %param.14), channel_id=1, replica_groups=mesh['dp'=8,'tensor'=4] {'dp'}, dimensions={0}, use_global_device_ids=true | all-gather | bytes 589824 | tf_op jit(solution)/shard_map/all_gather | solution.py:33
  43.8 26.8 %all-gather.2.cloned.1.call-done = bf16[7168,192]{0,1:T(8,128)(2,1)} async-done(((bf16[896,192]{0,1:T(8,128)(2,1)}), bf16[7168,192]{0,1:T(8,128)(2,1)}) %all-gather.2.cloned.1.call-update) | async-done | bytes 2752528 | tf_op jit(solution)/shard_map/all_gather | solution.py:22
  70.6 0.0 copy-start.4
  70.6 0.0 copy-start.6
  70.6 0.0 copy-start.7
  70.6 7.6 %fusion.16 = f32[256,320]{0,1:T(8,128)S(1)} fusion(bf16[256,7168]{1,0:T(8,128)(2,1)} %param.12, bf16[256,7168]{1,0:T(8,128)(2,1)} %param.13, bf16[256,7168]{1,0:T(8,128)(2,1)} %param.11, bf16[7168,192]{0,1:T(8,128)(2,1)} %all-gather.2.cloned.1.call-done), kind=kOutput, calls=%fused_computation.23 | convolution fusion | flops 258736128 | bytes 11993088 | tf_op jit(solution)/shard_map/dot_general | solution.py:26
  78.2 0.0 copy-done.4
  78.2 0.0 copy-done.6
  78.2 0.0 copy-done.7
  78.2 0.0 copy-start.5
  78.2 2.2 %fusion.22 = f32[256,320]{0,1:T(8,128)S(1)} fusion(f32[256,320]{0,1:T(8,128)S(1)} %fusion.16, bf16[256,7168]{1,0:T(8,128)(2,1)S(1)} %copy-done.6, bf16[256,7168]{1,0:T(8,128)(2,1)S(1)} %copy-done.4, bf16[7168,192]{0,1:T(8,128)(2,1)S(1)} %copy-done.7), kind=kOutput, calls=%fused_computation.25 | convolution fusion | flops 249561088 | bytes 8323072 | tf_op jit(solution)/shard_map/dot_general | solution.py:26
  80.5 0.0 copy-done.5
  80.5 0.0 copy-start.1
  80.5 2.3 %fusion.19 = f32[256,320]{0,1:T(8,128)S(1)} fusion(f32[256,320]{0,1:T(8,128)S(1)} %fusion.22, bf16[256,7168]{1,0:T(8,128)(2,1)S(1)} %copy-done.5, bf16[256,7168]{1,0:T(8,128)(2,1)S(1)} %copy-done.6, bf16[7168,192]{0,1:T(8,128)(2,1)S(1)} %copy-done.7), kind=kOutput, calls=%fused_computation.24 | convolution fusion | flops 249561088 | bytes 8323072 | tf_op jit(solution)/shard_map/dot_general | solution.py:26
  82.8 0.0 copy-done
  82.8 0.5 convolution_dynamic-update-slice_fusion.1
  83.2 0.0 copy-done.1
  83.3 0.6 convolution_dynamic-update-slice_fusion
  83.9 0.2 copy.12
  84.1 0.0 copy-start.2
  84.1 0.0 copy-start.3
  84.1 2.1 %gather_fusion = f32[768,320]{1,0:T(8,128)S(1)} fusion(f32[256,320]{1,0:T(8,128)S(1)} %copy.12, s32[1024]{0:T(1024)S(1)} %pad_clamp_fusion), kind=kCustom, calls=%fused_computation | custom fusion | bytes 1969152 | tf_op jit(solution)/shard_map/jit(_take)/gather | solution.py:55
  86.2 1.3 %select_multiply_fusion = f32[768,320]{1,0:T(8,128)} fusion(f32[768,320]{1,0:T(8,128)S(1)} %gather_fusion, f32[768]{0:T(1024)S(1)} %convert_element_type.41, pred[768]{0:T(1024)(128)(4,1)S(1)} %get-tuple-element.7), kind=kLoop, calls=%fused_computation.20 | loop fusion | flops 491520 | bytes 1969920 | tf_op jit(solution)/shard_map/mul | solution.py:55
  87.5 0.0 reduce-scatter.2.cloned.1.call-update
  87.5 0.0 copy-done.2
  87.6 0.0 copy-done.3
  87.6 0.6 fusion.45
  88.2 0.6 compare_convert_fusion
  88.9 22.9 %reduce-scatter.2.cloned.1.call-done = f32[192,320]{1,0:T(8,128)} async-done(((f32[768,320]{1,0:T(8,128)}), f32[192,320]{1,0:T(8,128)}) %reduce-scatter.2.cloned.1.call-update) | async-done | bytes 245776 | tf_op jit(solution)/shard_map/reduce_scatter | solution.py:54
  111.8 1.3 %convolution_bitcast_fusion = f32[1,64,64]{2,1,0:T(8,128)S(1)} fusion(f32[192,320]{1,0:T(8,128)} %reduce-scatter.2.cloned.1.call-done, f32[192]{0:T(256)S(1)} %compare_convert_fusion), kind=kOutput, calls=%fused_computation.26 | convolution fusion | flops 9449472 | bytes 213760 | tf_op jit(solution)/shard_map/ta,tb->ab/dot_general | solution.py:70
  113.1 1.4 %convolution_bitcast_fusion.1 = f32[1,64,64]{2,1,0:T(8,128)S(1)} fusion(f32[192,320]{1,0:T(8,128)} %reduce-scatter.2.cloned.1.call-done, f32[192]{0:T(256)S(1)} %compare_convert_fusion), kind=kOutput, calls=%fused_computation.27 | convolution fusion | flops 9449472 | bytes 213760 | tf_op jit(solution)/shard_map/ta,tb->ab/dot_general | solution.py:70
  114.5 1.3 %convolution_bitcast_fusion.2 = f32[1,64,64]{2,1,0:T(8,128)S(1)} fusion(f32[192,320]{1,0:T(8,128)} %reduce-scatter.2.cloned.1.call-done, f32[192]{0:T(256)S(1)} %compare_convert_fusion), kind=kOutput, calls=%fused_computation.28 | convolution fusion | flops 9449472 | bytes 213760 | tf_op jit(solution)/shard_map/ta,tb->ab/dot_general | solution.py:70
  115.9 0.7 reshape.85
  (6 shorter events, 0.1 us)
Async XLA Ops:
  6.5 76.2 %copy-start = (bf16[256,2048]{1,0:T(8,128)(2,1)S(1)}, bf16[256,2048]{1,0:T(8,128)(2,1)}, u32[]{:S(2)}) copy-start(bf16[256,2048]{1,0:T(8,128)(2,1)} %param.9) | copy-start | bytes 3145732
  6.5 64.1 %all-gather.2.cloned.1.call-start = ((), (), s32[]{:S(2)}) async-start(), calls=%async_computation.1 | async-start | bytes 3096576 | tf_op jit(solution)/shard_map/all_gather | solution.py:22
  7.3 104.5 %reduce-scatter.2.cloned.1.call-start = ((), (), s32[]{:S(2)}) async-start(), calls=%async_computation.2 | async-start | bytes 1474560 | tf_op jit(solution)/shard_map/reduce_scatter | solution.py:54
  70.6 7.6 %copy-start.4 = (bf16[256,7168]{1,0:T(8,128)(2,1)S(1)}, bf16[256,7168]{1,0:T(8,128)(2,1)}, u32[]{:S(2)}) copy-start(bf16[256,7168]{1,0:T(8,128)(2,1)} %param.13) | copy-start | bytes 11010052
  70.6 7.6 %copy-start.6 = (bf16[256,7168]{1,0:T(8,128)(2,1)S(1)}, bf16[256,7168]{1,0:T(8,128)(2,1)}, u32[]{:S(2)}) copy-start(bf16[256,7168]{1,0:T(8,128)(2,1)} %param.11) | copy-start | bytes 11010052
  70.6 7.6 %copy-start.7 = (bf16[7168,192]{0,1:T(8,128)(2,1)S(1)}, bf16[7168,192]{0,1:T(8,128)(2,1)}, u32[]{:S(2)}) copy-start(bf16[7168,192]{0,1:T(8,128)(2,1)} %all-gather.2.cloned.1.call-done) | copy-start | bytes 8257540
  78.2 2.3 %copy-start.5 = (bf16[256,7168]{1,0:T(8,128)(2,1)S(1)}, bf16[256,7168]{1,0:T(8,128)(2,1)}, u32[]{:S(2)}) copy-start(bf16[256,7168]{1,0:T(8,128)(2,1)} %param.12) | copy-start | bytes 11010052
  80.5 2.8 %copy-start.1 = (bf16[256,2048]{1,0:T(8,128)(2,1)S(1)}, bf16[256,2048]{1,0:T(8,128)(2,1)}, u32[]{:S(2)}) copy-start(bf16[256,2048]{1,0:T(8,128)(2,1)} %param.10) | copy-start | bytes 3145732
  84.1 3.5 %copy-start.2 = (s32[1,4]{1,0:T(1,128)S(1)}, s32[1,4]{1,0:T(1,128)}, u32[]{:S(2)}) copy-start(s32[1,4]{1,0:T(1,128)} %param.16) | copy-start | bytes 52
  84.1 3.5 %copy-start.3 = (s32[1,4]{1,0:T(1,128)S(1)}, s32[1,4]{1,0:T(1,128)}, u32[]{:S(2)}) copy-start(s32[1,4]{1,0:T(1,128)} %param.17) | copy-start | bytes 52
Sparse Core Ops, SparseCore 0:
  9.5 61.0 all-gather.1
  87.7 24.0 reduce-scatter.1
where the time goes:
time: 124 us; the launch traced here: 123 us
  waiting for transfers between devices  50.5 us (41%)
  blocking collectives  34.1 us (28%)
  matrix products  17.3 us (14%)
  between operations  13.6 us (11%)
  other arithmetic  4.88 us (4%)
  local copies, waits for them, and re-layouts  3.07 us (2%)
    all_gather x1, blocking collectives, per_device(): block_rows = lax.all_gather(proj_model, 'dp', axis=0, tiled=True)  34.1 us
    all_gather x1, waiting for transfers between devices, per_device(): block_rows = lax.all_gather(proj_hidden, 'dp', axis=0, tiled=True)  26.8 us
    reduce_scatter x1, waiting for transfers between devices, per_device(): lax.psum_scatter(jnp.take(partial_value, picked, axis=0) * valid[:, None]...  22.9 us
    dot_general x3, matrix products, per_device(): jnp.dot(source, block_rows[:, column * rank_width:(column + 1) * rank_wid...  12.1 us
    dot_general x3, matrix products, per_device(): jnp.einsum('ta,tb->ab', left_side, block_of(right_index), precision=lax.P...  4.07 us
  transfers between devices with their start and end apart: 2, of which 2 were waited for; matrix products, arithmetic and copies ran while one was open for 3% of the time, Pallas kernels for 0%

commit v1 on v0

--- a/solution.py
+++ b/solution.py
@@ -1,7 +1,335 @@
+import functools
+import math
+
 import jax
 import jax.numpy as jnp
 from jax import lax
+from jax.experimental import pallas as pl
+from jax.experimental.pallas import tpu as pltpu
 from jax.sharding import PartitionSpec as P
+
+MESH = pl.DeviceIdType.MESH
+NT = (((1,), (1,)), ((), ()))
+TN = (((0,), (0,)), ((), ()))
+F32 = jnp.float32
+BF16 = jnp.bfloat16
+ROWS = 32
+
+
+def kernel(
+    nz, nx, ny,
+    inp_h, og_h, gp_h, up_h, hg_h, pm_h, wt_h, lens, owns,
+    out,
+    raw, act, inp_v, og_v, pmb, whb, wgb, acc, part, rx1, chip, sx2, rx2, full, fs,
+    raw_sem, io_sem, own_sem, recv, s_up, s_dn, s_x, r_sem, t_sem, r2_sem, t2_sem,
+):
+    ndp = nz * nx
+    me = lax.axis_index("dp")
+    t = lax.axis_index("tensor")
+    z, x = me // nx, me % nx
+    y, c = t // 2, t % 2
+    mate = y * 2 + 1 - c
+    units = wt_h.shape[1]
+    feats = pm_h.shape[0]
+    toks = inp_h.shape[0]
+    half = toks // 2
+    sources = (gp_h, up_h, hg_h)
+
+    def raw_copy(block, slot, q):
+        cols = pl.ds(pl.multiple_of(block * units, 128), units)
+        return pltpu.make_async_copy(sources[q].at[:, cols], raw.at[slot, q], raw_sem.at[slot, q])
+
+    for q in range(3):
+        raw_copy(0, 0, q).start()
+    io = (pltpu.make_async_copy(inp_h, inp_v, io_sem.at[0]),
+          pltpu.make_async_copy(og_h, og_v, io_sem.at[1]))
+    bufs = (pmb, whb, wgb)
+    own = (pm_h, wt_h.at[pl.ds(128, 64), :], wt_h.at[pl.ds(0, 128), :])
+
+    barrier = pltpu.get_barrier_semaphore()
+
+    def greet(d, s):
+        pl.semaphore_signal(barrier, inc=1, device_id=(d, s), device_id_type=MESH)
+
+    for j in range(1, nx):
+        greet(z * nx + (x + j) % nx, t)
+    for j in range(1, ny):
+        greet(me, ((y + j) % ny) * 2 + c)
+    greet(me, mate)
+
+    @pl.when(z < nz - 1)
+    def _():
+        greet(me + nx, t)
+
+    @pl.when(z > 0)
+    def _():
+        greet(me - nx, t)
+
+    pl.semaphore_wait(
+        barrier, nx + ny - 1 + (z < nz - 1).astype(jnp.int32) + (z > 0).astype(jnp.int32)
+    )
+
+    def remote(p, src, slot, sem, d):
+        return pltpu.make_async_remote_copy(
+            src_ref=src, dst_ref=bufs[p].at[slot], send_sem=sem, recv_sem=recv.at[slot, p],
+            device_id=(d, t), device_id_type=MESH,
+        )
+
+    def across(p, src, slot, j):
+        return remote(p, src, slot, s_x.at[slot, p, j - 1], z * nx + (x + j) % nx)
+
+    def upward(p, src, slot):
+        return remote(p, src, slot, s_up.at[slot, p], me + nx)
+
+    def downward(p, src, slot):
+        return remote(p, src, slot, s_dn.at[slot, p], me - nx)
+
+    for p in range(3):
+        @pl.when(z < nz - 1)
+        def _():
+            upward(p, own[p], me).start()
+
+        @pl.when(z > 0)
+        def _():
+            downward(p, own[p], me).start()
+
+        for j in range(1, nx):
+            across(p, own[p], me, j).start()
+    keep = [pltpu.make_async_copy(own[p], bufs[p].at[me], own_sem.at[p]) for p in range(3)]
+    for p in range(3):
+        keep[p].start()
+    for copy in io:
+        copy.start()
+    acc[...] = jnp.zeros_like(acc)
+
+    def elementwise(block, carry):
+        slot = block % 2
+
+        @pl.when(block + 1 < ndp)
+        def _():
+            for q in range(3):
+                raw_copy(block + 1, 1 - slot, q).start()
+
+        for q in range(3):
+            raw_copy(block, slot, q).wait()
+
+        def some(i, carry):
+            rows = pl.ds(pl.multiple_of(i * ROWS, ROWS), ROWS)
+            gate = raw[slot, 0, rows, :].astype(F32)
+            up = raw[slot, 1, rows, :].astype(F32)
+            grad = raw[slot, 2, rows, :].astype(F32)
+            sig = 0.5 * jnp.tanh(0.5 * gate) + 0.5
+            silu = gate * sig
+            act[0, block, rows, :] = (grad * up * (sig + silu * (1.0 - sig))).astype(BF16)
+            act[1, block, rows, :] = (grad * silu).astype(BF16)
+            act[2, block, rows, :] = (silu * up).astype(BF16)
+            return carry
+
+        lax.fori_loop(0, toks // ROWS, some, 0)
+        return carry
+
+    lax.fori_loop(0, ndp, elementwise, 0)
+    for copy in io:
+        copy.wait()
+    for p in range(3):
+        keep[p].wait()
+
+    def dots(slot):
+        cols = pl.ds(pl.multiple_of(slot * feats, 128), feats)
+        weights = pmb[slot]
+        acc[0] += lax.dot_general(act[0, slot], wgb[slot], NT, preferred_element_type=F32)
+        acc[1] += lax.dot_general(act[1, slot], wgb[slot], NT, preferred_element_type=F32)
+        acc[2] += jnp.dot(inp_v[:, cols], weights, preferred_element_type=F32)
+        acc[3] += jnp.dot(og_v[:, cols], weights, preferred_element_type=F32)
+        acc[4, :, pl.ds(0, 64)] += lax.dot_general(
+            act[2, slot], whb[slot], NT, preferred_element_type=F32
+        )
+
+    near = jnp.minimum(z, nz - 1 - z)
+
+    def plane(i):
+        k = (i + 1) // 2
+        paired = jnp.where(i % 2 == 1, z + k, z - k)
+        far = jnp.where(z < nz - 1 - z, z + i - near, z - i + near)
+        return jnp.where(i <= 2 * near, paired, far)
+
+    def step(i, carry):
+        @pl.when(i < nz)
+        def _():
+            src_z = plane(i)
+            slot = src_z * nx + x
+
+            @pl.when(i > 0)
+            def _():
+                for p in range(3):
+                    block = bufs[p].at[slot]
+                    across(p, block, slot, 1).wait_recv()
+
+                    @pl.when((src_z < z) & (z < nz - 1))
+                    def _():
+                        upward(p, block, slot).start()
+
+                    @pl.when((src_z > z) & (z > 0))
+                    def _():
+                        downward(p, block, slot).start()
+
+                    for j in range(1, nx):
+                        across(p, block, slot, j).start()
+
+            dots(slot)
+
+        @pl.when(i > 0)
+        def _():
+            for j in range(1, nx):
+                slot = plane(i - 1) * nx + (x + j) % nx
+                for p in range(3):
+                    across(p, bufs[p].at[slot], slot, 1).wait_recv()
+                dots(slot)
+
+        return carry
+
+    lax.fori_loop(0, nz + 1, step, 0)
+
+    low = lax.broadcasted_iota(jnp.int32, (toks, 128), 1) < 64
+    part[0] = jnp.where(low, acc[0], acc[1])
+    part[1] = jnp.where(low, acc[2], acc[3])
+    part[2] = acc[4]
+    mine = pl.ds(pl.multiple_of(c * half, half), half)
+    other = pl.ds(pl.multiple_of((1 - c) * half, half), half)
+    first = pltpu.make_async_remote_copy(
+        src_ref=part.at[:, other, :], dst_ref=rx1, send_sem=t_sem.at[0], recv_sem=r_sem.at[0],
+        device_id=(me, mate), device_id_type=MESH,
+    )
+    first.start()
+    first.wait_recv()
+    both = part[:, mine, :] + rx1[...]
+    chip[...] = both
+    sx2[...] = both.astype(BF16)
+    swaps = [
+        pltpu.make_async_remote_copy(
+            src_ref=sx2, dst_ref=rx2.at[j - 1], send_sem=t2_sem.at[j - 1],
+            recv_sem=r2_sem.at[j - 1],
+            device_id=(me, ((y + j) % ny) * 2 + c), device_id_type=MESH,
+        )
+        for j in range(1, ny)
+    ]
+    for copy in swaps:
+        copy.start()
+    for copy in swaps:
+        copy.wait_recv()
+    whole = chip[...]
+    for j in range(1, ny):
+        whole = whole + rx2[j - 1].astype(F32)
+    full[c] = whole
+    last = pltpu.make_async_remote_copy(
+        src_ref=full.at[c], dst_ref=full.at[c], send_sem=t_sem.at[1], recv_sem=r_sem.at[1],
+        device_id=(me, mate), device_id_type=MESH,
+    )
+    last.start()
+
+    start, length, seen = jnp.int32(0), jnp.int32(0), jnp.int32(0)
+    for e in range(2 * ny):
+        hit = owns[0, e] == t
+        start = jnp.where(hit, seen, start)
+        length = jnp.where(hit, lens[0, e], length)
+        seen = seen + lens[0, e]
+    last.wait_recv()
+
+    places = lax.broadcasted_iota(jnp.int32, (half, 128), 0)
+    pair_one = jnp.zeros((128, 128), F32)
+    pair_two = jnp.zeros((128, 128), F32)
+    for h in range(2):
+        token = places + h * half
+        inside = (token >= start) & (token < start + length)
+        model = full[h, 1]
+        pair_one += lax.dot_general(
+            jnp.where(inside, full[h, 0], 0.0), model, TN,
+            precision=lax.Precision.HIGHEST, preferred_element_type=F32,
+        )
+        pair_two += lax.dot_general(
+            jnp.where(inside, model, 0.0), full[h, 2], TN,
+            precision=lax.Precision.HIGHEST, preferred_element_type=F32,
+        )
+    fs[pl.ds(0, 128), :] = pair_one
+    fs[pl.ds(128, 64), :] = pair_two[64:, :]
+    even = fs[pl.ds(0, 96, stride=2), :]
+    odd = fs[pl.ds(1, 96, stride=2), :]
+    out[...] = jnp.concatenate([even[:, :64], odd[:, :64]], axis=1)
+
+    first.wait_send()
+    last.wait_send()
+    for copy in swaps:
+        copy.wait_send()
+
+    def drain(src_z, carry):
+        slot = src_z * nx + x
+        for p in range(3):
+            block = bufs[p].at[slot]
+
+            @pl.when((src_z <= z) & (z < nz - 1))
+            def _():
+                upward(p, block, slot).wait_send()
+
+            @pl.when((src_z >= z) & (z > 0))
+            def _():
+                downward(p, block, slot).wait_send()
+
+            for j in range(1, nx):
+                across(p, block, slot, j).wait_send()
+        return carry
+
+    lax.fori_loop(0, nz, drain, 0)
+
+
+def fused(
+    nz, nx, ny,
+    inputs, out_grads, gate_pre, up_pre, hidden_grad, proj_model, proj_hidden, lengths, owners,
+):
+    ndp = nz * nx
+    toks, wide = inputs.shape
+    units, feats = proj_hidden.shape[0], proj_model.shape[0]
+    half = toks // 2
+    hbm = pl.BlockSpec(memory_space=pltpu.HBM)
+    smem = pl.BlockSpec(memory_space=pltpu.SMEM)
+    dma = pltpu.SemaphoreType.DMA
+    out = pl.pallas_call(
+        functools.partial(kernel, nz, nx, ny),
+        out_shape=jax.ShapeDtypeStruct((96, 128), F32),
+        in_specs=[hbm] * 7 + [smem] * 2,
+        out_specs=pl.BlockSpec(memory_space=pltpu.VMEM),
+        scratch_shapes=[
+            pltpu.VMEM((2, 3, toks, units), BF16),
+            pltpu.VMEM((3, ndp, toks, units), BF16),
+            pltpu.VMEM((toks, wide), BF16),
+            pltpu.VMEM((toks, wide), BF16),
+            pltpu.VMEM((ndp, feats, 128), BF16),
+            pltpu.VMEM((ndp, 64, units), BF16),
+            pltpu.VMEM((ndp, 128, units), BF16),
+            pltpu.VMEM((5, toks, 128), F32),
+            pltpu.VMEM((3, toks, 128), F32),
+            pltpu.VMEM((3, half, 128), F32),
+            pltpu.VMEM((3, half, 128), F32),
+            pltpu.VMEM((3, half, 128), BF16),
+            pltpu.VMEM((ny - 1, 3, half, 128), BF16),
+            pltpu.VMEM((2, 3, half, 128), F32),
+            pltpu.VMEM((192, 128), F32),
+            dma((2, 3)),
+            dma((2,)),
+            dma((3,)),
+            dma((ndp, 3)),
+            dma((ndp, 3)),
+            dma((ndp, 3)),
+            dma((ndp, 3, nx - 1)),
+            dma((2,)),
+            dma((2,)),
+            dma((ny - 1,)),
+            dma((ny - 1,)),
+        ],
+        compiler_params=pltpu.CompilerParams(
+            collective_id=0, has_side_effects=True, vmem_limit_bytes=48 << 20
+        ),
+    )(inputs, out_grads, gate_pre, up_pre, hidden_grad, proj_model, proj_hidden.T, lengths, owners)
+    return out.reshape(1, 3 * 64 * 64)
 
 
 def per_device(
@@ -87,6 +415,16 @@
         P("dp", None),
     )
     out_specs = P(("dp", "tensor"), None)
+    ndp, ny = mesh.shape["dp"], mesh.shape["tensor"] // 2
+
+    def program(*args):
+        units, feats, rank_width = args[6].shape[0], args[5].shape[0], args[5].shape[1] // 2
+        nx = math.isqrt(ndp // 2)
+        fits = units % 128 == 0 and feats % 128 == 0 and rank_width == 64
+        if fits and ny > 1 and nx > 1 and ndp % nx == 0 and args[0].shape[0] % 64 == 0:
+            return fused(ndp // nx, nx, ny, *args)
+        return per_device(*args)
+
     return jax.shard_map(
-        per_device, mesh=mesh, in_specs=in_specs, out_specs=out_specs, check_vma=False
-    )
+        program, mesh=mesh, in_specs=in_specs, out_specs=out_specs, check_vma=False
+    )

time: 124 us -> 55.6 us (0.45)
  waiting for transfers between devices: 50.5 us -> 0 us
  Pallas kernels: 0 us -> 48.9 us
  blocking collectives: 34.1 us -> 0 us
  matrix products: 17.3 us -> 0 us
  between operations: 13.6 us -> 0.02 us
  other arithmetic: 4.88 us -> 0 us
  local copies, waits for them, and re-layouts: 3.07 us -> 6.2 us
    pallas_call x0 -> x1, Pallas kernels: none -> 48.9 us  [fused(): pl.pallas_call(functools.partial(kernel, nz, nx, ny), out_shape=jax.Shape...]
    all_gather x1 -> x0, blocking collectives: 34.1 us -> none  [per_device(): block_rows = lax.all_gather(proj_model, 'dp', axis=0, tiled=True)]
    all_gather x1 -> x0, waiting for transfers between devices: 26.8 us -> none  [per_device(): block_rows = lax.all_gather(proj_hidden, 'dp', axis=0, tiled=True)]
    reduce_scatter x1 -> x0, waiting for transfers between devices: 22.9 us -> none  [per_device(): lax.psum_scatter(jnp.take(partial_value, picked, axis=0) * valid[:, None]...]
    dot_general x8 -> x0, matrix products: 17.3 us -> none  [the longest x3 12.1 us: per_device(): jnp.dot(source, block_rows[:, column * rank_width:(column + 1) * rank_wid...]
    unnamed x16 -> x13, local copies, waits for them, and re-layouts: 0.04 us -> 6.2 us
    gather x1 -> x0, local copies, waits for them, and re-layouts: 2.13 us -> none  [per_device(): jnp.take(partial_value, picked, axis=0) * valid[:, None].astype(jnp.float32)]
    mul x2 -> x0, other arithmetic: 1.94 us -> none  [the longest x1 1.28 us: per_device(): jnp.take(partial_value, picked, axis=0) * valid[:, None].astype(jnp.float32)]
  transfers between devices with their start and end apart: 2 -> 0, of which waited for: 2 -> 0; matrix products, arithmetic and copies ran while one was open for 3% -> 0% of each run, Pallas kernels for 0% -> 0%
where the time goes in v1:
time: 55.6 us; the launch traced here: 55.2 us
  Pallas kernels  48.9 us (88%)
  local copies, waits for them, and re-layouts  6.2 us (11%)
    pallas_call x1, Pallas kernels, fused(): pl.pallas_call(functools.partial(kernel, nz, nx, ny), out_shape=jax.Shape...  48.9 us
    unnamed x13, local copies, waits for them, and re-layouts  6.2 us

profile of v1, /device:TPU:0, one launch (start us, length us, event | category | flops | bytes accessed | tf_op | source)
XLA Modules:
  0.0 55.2 jit_solution(16968268444084804543)
XLA Ops:
  0.0 0.0 copy-start
  0.0 1.2 %copy-done = bf16[256,2048]{1,0:T(8,128)(2,1)S(1)} copy-done((bf16[256,2048]{1,0:T(8,128)(2,1)S(1)}, bf16[256,2048]{1,0:T(8,128)(2,1)}, u32[]{:S(2)}) %copy-start) | copy-done | bytes 1048600
  1.2 0.0 copy-start.1
  1.2 1.2 %copy-done.1 = bf16[256,2048]{1,0:T(8,128)(2,1)S(1)} copy-done((bf16[256,2048]{1,0:T(8,128)(2,1)S(1)}, bf16[256,2048]{1,0:T(8,128)(2,1)}, u32[]{:S(2)}) %copy-start.1) | copy-done | bytes 1048600
  2.5 0.0 copy-start.2
  2.5 1.0 %copy-done.2 = bf16[896,192]{0,1:T(8,128)(2,1)S(1)} copy-done((bf16[896,192]{0,1:T(8,128)(2,1)S(1)}, bf16[896,192]{0,1:T(8,128)(2,1)}, u32[]{:S(2)}) %copy-start.2) | copy-done | bytes 344088
  3.4 0.0 copy-start.3
  3.4 0.8 %copy-done.3 = bf16[256,128]{1,0:T(8,128)(2,1)S(1)} copy-done((bf16[256,128]{1,0:T(8,128)(2,1)S(1)}, bf16[256,128]{1,0:T(8,128)(2,1)}, u32[]{:S(2)}) %copy-start.3) | copy-done | bytes 65560
  4.3 0.0 copy-start.4
  4.3 0.7 %copy-done.4 = s32[1,4]{1,0:T(1,128)S(1)} copy-done((s32[1,4]{1,0:T(1,128)S(1)}, s32[1,4]{1,0:T(1,128)}, u32[]{:S(2)}) %copy-start.4) | copy-done | bytes 40
  4.9 0.0 copy-start.5
  4.9 0.7 %copy-done.5 = s32[1,4]{1,0:T(1,128)S(1)} copy-done((s32[1,4]{1,0:T(1,128)S(1)}, s32[1,4]{1,0:T(1,128)}, u32[]{:S(2)}) %copy-start.5) | copy-done | bytes 40
  5.6 48.9 %shard_map.91 = f32[96,128]{1,0:T(8,128)S(1)} custom-call(bf16[256,2048]{1,0:T(8,128)(2,1)S(1)} %copy-done, bf16[256,2048]{1,0:T(8,128)(2,1)S(1)} %copy-done.1, bf16[256,7168]{1,0:T(8,128)(2,1)} %gp_h.1, bf16[256,7168]{1,0:T(8,128)(2,1)} %up_h.1, bf16[256,7168]{1,0:T(8,128)(2,1)} %hg_h.1, bf16[256,128]{1,0:T(8,128)(2,1)S(1)} %copy-done.3, ...), custom_call_target="tpu_custom_call" | custom-call | tf_op jit(solution)/shard_map/pallas_call | solution.py:295
  54.5 0.6 %copy.11 = f32[1,12288]{1,0:T(1,128)} copy(f32[1,12288]{1,0:T(1,128)S(1)} %bitcast.3) | data formatting | bytes 98304
Async XLA Ops:
  0.0 1.2 %copy-start = (bf16[256,2048]{1,0:T(8,128)(2,1)S(1)}, bf16[256,2048]{1,0:T(8,128)(2,1)}, u32[]{:S(2)}) copy-start(bf16[256,2048]{1,0:T(8,128)(2,1)} %inp_h.1) | copy-start | bytes 3145732
  1.2 1.2 %copy-start.1 = (bf16[256,2048]{1,0:T(8,128)(2,1)S(1)}, bf16[256,2048]{1,0:T(8,128)(2,1)}, u32[]{:S(2)}) copy-start(bf16[256,2048]{1,0:T(8,128)(2,1)} %og_h.1) | copy-start | bytes 3145732
  2.5 1.0 %copy-start.2 = (bf16[896,192]{0,1:T(8,128)(2,1)S(1)}, bf16[896,192]{0,1:T(8,128)(2,1)}, u32[]{:S(2)}) copy-start(bf16[896,192]{0,1:T(8,128)(2,1)} %param.15) | copy-start | bytes 1032196
  3.4 0.8 %copy-start.3 = (bf16[256,128]{1,0:T(8,128)(2,1)S(1)}, bf16[256,128]{1,0:T(8,128)(2,1)}, u32[]{:S(2)}) copy-start(bf16[256,128]{1,0:T(8,128)(2,1)} %pm_h.1) | copy-start | bytes 196612
  4.3 0.7 %copy-start.4 = (s32[1,4]{1,0:T(1,128)S(1)}, s32[1,4]{1,0:T(1,128)}, u32[]{:S(2)}) copy-start(s32[1,4]{1,0:T(1,128)} %lens.1) | copy-start | bytes 52
  4.9 0.7 %copy-start.5 = (s32[1,4]{1,0:T(1,128)S(1)}, s32[1,4]{1,0:T(1,128)}, u32[]{:S(2)}) copy-start(s32[1,4]{1,0:T(1,128)} %owns.1) | copy-start | bytes 52

commit v2 on v1

--- a/solution.py
+++ b/solution.py
@@ -14,13 +14,15 @@
 F32 = jnp.float32
 BF16 = jnp.bfloat16
 ROWS = 32
+ALONG = 2
+PIECES = ((128, 64), (0, 64), (64, 64))
 
 
 def kernel(
     nz, nx, ny,
     inp_h, og_h, gp_h, up_h, hg_h, pm_h, wt_h, lens, owns,
     out,
-    raw, act, inp_v, og_v, pmb, whb, wgb, acc, part, rx1, chip, sx2, rx2, full, fs,
+    raw, act, inp_v, og_v, pmb, wtb, acc, part, rx1, chip, sx2, rx2, full, fs,
     raw_sem, io_sem, own_sem, recv, s_up, s_dn, s_x, r_sem, t_sem, r2_sem, t2_sem,
 ):
     ndp = nz * nx
@@ -43,8 +45,11 @@
         raw_copy(0, 0, q).start()
     io = (pltpu.make_async_copy(inp_h, inp_v, io_sem.at[0]),
           pltpu.make_async_copy(og_h, og_v, io_sem.at[1]))
-    bufs = (pmb, whb, wgb)
-    own = (pm_h, wt_h.at[pl.ds(128, 64), :], wt_h.at[pl.ds(0, 128), :])
+    pieces = 1 + len(PIECES)
+    own = [pm_h] + [wt_h.at[pl.ds(row, n), :] for row, n in PIECES]
+
+    def held(p, slot):
+        return pmb.at[slot] if p == 0 else wtb.at[slot, pl.ds(*PIECES[p - 1]), :]
 
     barrier = pltpu.get_barrier_semaphore()
 
@@ -71,7 +76,7 @@
 
     def remote(p, src, slot, sem, d):
         return pltpu.make_async_remote_copy(
-            src_ref=src, dst_ref=bufs[p].at[slot], send_sem=sem, recv_sem=recv.at[slot, p],
+            src_ref=src, dst_ref=held(p, slot), send_sem=sem, recv_sem=recv.at[slot, p],
             device_id=(d, t), device_id_type=MESH,
         )
 
@@ -84,7 +89,7 @@
     def downward(p, src, slot):
         return remote(p, src, slot, s_dn.at[slot, p], me - nx)
 
-    for p in range(3):
+    for p in range(pieces):
         @pl.when(z < nz - 1)
         def _():
             upward(p, own[p], me).start()
@@ -95,8 +100,8 @@
 
         for j in range(1, nx):
             across(p, own[p], me, j).start()
-    keep = [pltpu.make_async_copy(own[p], bufs[p].at[me], own_sem.at[p]) for p in range(3)]
-    for p in range(3):
+    keep = [pltpu.make_async_copy(own[p], held(p, me), own_sem.at[p]) for p in range(pieces)]
+    for p in range(pieces):
         keep[p].start()
     for copy in io:
         copy.start()
@@ -131,19 +136,31 @@
     lax.fori_loop(0, ndp, elementwise, 0)
     for copy in io:
         copy.wait()
-    for p in range(3):
+    for p in range(pieces):
         keep[p].wait()
 
     def dots(slot):
         cols = pl.ds(pl.multiple_of(slot * feats, 128), feats)
         weights = pmb[slot]
-        acc[0] += lax.dot_general(act[0, slot], wgb[slot], NT, preferred_element_type=F32)
-        acc[1] += lax.dot_general(act[1, slot], wgb[slot], NT, preferred_element_type=F32)
+        pair = wtb[slot, pl.ds(0, 128), :]
+        acc[0] += lax.dot_general(act[0, slot], pair, NT, preferred_element_type=F32)
+        acc[1] += lax.dot_general(act[1, slot], pair, NT, preferred_element_type=F32)
         acc[2] += jnp.dot(inp_v[:, cols], weights, preferred_element_type=F32)
         acc[3] += jnp.dot(og_v[:, cols], weights, preferred_element_type=F32)
         acc[4, :, pl.ds(0, 64)] += lax.dot_general(
-            act[2, slot], whb[slot], NT, preferred_element_type=F32
-        )
+            act[2, slot], wtb[slot, pl.ds(128, 64), :], NT, preferred_element_type=F32
+        )
+
+    def along(p, src_z):
+        low_end = (src_z == 0) & ((z == 1) | (z == nz - 1))
+        high_end = (src_z == nz - 1) & ((z == nz - 2) | (z == 0))
+        return low_end | high_end if p < ALONG else src_z < 0
+
+    def passes_up(p, src_z):
+        return (src_z == 0) & ((z == 0) | (z == nz - 2)) if p < ALONG else src_z < 0
+
+    def passes_down(p, src_z):
+        return (src_z == nz - 1) & ((z == nz - 1) | (z == 1)) if p < ALONG else src_z < 0
 
     near = jnp.minimum(z, nz - 1 - z)
 
@@ -161,8 +178,8 @@
 
             @pl.when(i > 0)
             def _():
-                for p in range(3):
-                    block = bufs[p].at[slot]
+                for p in range(pieces):
+                    block = held(p, slot)
                     across(p, block, slot, 1).wait_recv()
 
                     @pl.when((src_z < z) & (z < nz - 1))
@@ -173,17 +190,30 @@
                     def _():
                         downward(p, block, slot).start()
 
-                    for j in range(1, nx):
-                        across(p, block, slot, j).start()
+                    @pl.when(jnp.logical_not(along(p, src_z)))
+                    def _():
+                        for j in range(1, nx):
+                            across(p, block, slot, j).start()
 
             dots(slot)
 
         @pl.when(i > 0)
         def _():
+            src_z = plane(i - 1)
             for j in range(1, nx):
-                slot = plane(i - 1) * nx + (x + j) % nx
-                for p in range(3):
-                    across(p, bufs[p].at[slot], slot, 1).wait_recv()
+                slot = src_z * nx + (x + j) % nx
+                for p in range(pieces):
+                    block = held(p, slot)
+                    across(p, block, slot, 1).wait_recv()
+
+                    @pl.when(passes_up(p, src_z))
+                    def _():
+                        upward(p, block, slot).start()
+
+                    @pl.when(passes_down(p, src_z))
+                    def _():
+                        downward(p, block, slot).start()
+
                 dots(slot)
 
         return carry
@@ -263,8 +293,8 @@
 
     def drain(src_z, carry):
         slot = src_z * nx + x
-        for p in range(3):
-            block = bufs[p].at[slot]
+        for p in range(pieces):
+            block = held(p, slot)
 
             @pl.when((src_z <= z) & (z < nz - 1))
             def _():
@@ -274,8 +304,22 @@
             def _():
                 downward(p, block, slot).wait_send()
 
+            @pl.when(jnp.logical_not(along(p, src_z)))
+            def _():
+                for j in range(1, nx):
+                    across(p, block, slot, j).wait_send()
+
             for j in range(1, nx):
-                across(p, block, slot, j).wait_send()
+                slot_b = src_z * nx + (x + j) % nx
+                block_b = held(p, slot_b)
+
+                @pl.when(passes_up(p, src_z))
+                def _():
+                    upward(p, block_b, slot_b).wait_send()
+
+                @pl.when(passes_down(p, src_z))
+                def _():
+                    downward(p, block_b, slot_b).wait_send()
         return carry
 
     lax.fori_loop(0, nz, drain, 0)
@@ -303,8 +347,7 @@
             pltpu.VMEM((toks, wide), BF16),
             pltpu.VMEM((toks, wide), BF16),
             pltpu.VMEM((ndp, feats, 128), BF16),
-            pltpu.VMEM((ndp, 64, units), BF16),
-            pltpu.VMEM((ndp, 128, units), BF16),
+            pltpu.VMEM((ndp, 192, units), BF16),
             pltpu.VMEM((5, toks, 128), F32),
             pltpu.VMEM((3, toks, 128), F32),
             pltpu.VMEM((3, half, 128), F32),
@@ -315,18 +358,18 @@
             pltpu.VMEM((192, 128), F32),
             dma((2, 3)),
             dma((2,)),
-            dma((3,)),
-            dma((ndp, 3)),
-            dma((ndp, 3)),
-            dma((ndp, 3)),
-            dma((ndp, 3, nx - 1)),
+            dma((1 + len(PIECES),)),
+            dma((ndp, 1 + len(PIECES))),
+            dma((ndp, 1 + len(PIECES))),
+            dma((ndp, 1 + len(PIECES))),
+            dma((ndp, 1 + len(PIECES), nx - 1)),
             dma((2,)),
             dma((2,)),
             dma((ny - 1,)),
             dma((ny - 1,)),
         ],
         compiler_params=pltpu.CompilerParams(
-            collective_id=0, has_side_effects=True, vmem_limit_bytes=48 << 20
+            collective_id=0, has_side_effects=True, vmem_limit_bytes=62 << 20
         ),
     )(inputs, out_grads, gate_pre, up_pre, hidden_grad, proj_model, proj_hidden.T, lengths, owners)
     return out.reshape(1, 3 * 64 * 64)
@@ -421,7 +464,7 @@
         units, feats, rank_width = args[6].shape[0], args[5].shape[0], args[5].shape[1] // 2
         nx = math.isqrt(ndp // 2)
         fits = units % 128 == 0 and feats % 128 == 0 and rank_width == 64
-        if fits and ny > 1 and nx > 1 and ndp % nx == 0 and args[0].shape[0] % 64 == 0:
+        if fits and ny > 1 and nx > 1 and ndp // nx > 3 and ndp % nx == 0 and args[0].shape[0] % 64 == 0:
             return fused(ndp // nx, nx, ny, *args)
         return per_device(*args)
 

time: 55.6 us -> 50.5 us (0.908)
  local copies, waits for them, and re-layouts: 6.2 us -> 1.42 us
    unnamed x13 -> x1, local copies, waits for them, and re-layouts: 6.2 us -> 1.42 us
where the time goes in v2:
time: 50.5 us; the launch traced here: 50.2 us
  Pallas kernels  48.8 us (97%)
  local copies, waits for them, and re-layouts  1.42 us (3%)
    pallas_call x1, Pallas kernels, fused(): pl.pallas_call(functools.partial(kernel, nz, nx, ny), out_shape=jax.Shape...  48.8 us
    unnamed x1, local copies, waits for them, and re-layouts  1.42 us

profile of v2, /device:TPU:0, one launch (start us, length us, event | category | flops | bytes accessed | tf_op | source)
XLA Modules:
  0.0 50.2 jit_solution(16543241874574696217)
XLA Ops:
  0.0 48.8 %shard_map.91 = f32[96,128]{1,0:T(8,128)} custom-call(bf16[256,2048]{1,0:T(8,128)(2,1)} %inp_h.1, bf16[256,2048]{1,0:T(8,128)(2,1)} %og_h.1, bf16[256,7168]{1,0:T(8,128)(2,1)} %gp_h.1, bf16[256,7168]{1,0:T(8,128)(2,1)} %up_h.1, bf16[256,7168]{1,0:T(8,128)(2,1)} %hg_h.1, bf16[256,128]{1,0:T(8,128)(2,1)} %pm_h.1, bf16[192,896]{1,0:T(8,128)(2,1)} %bitcast.2, ...), custom_call_target="tpu_custom_call" | custom-call | tf_op jit(solution)/shard_map/pallas_call | solution.py:339
  48.8 1.4 %copy.11 = f32[1,12288]{1,0:T(1,128)} copy(f32[1,12288]{1,0:T(1,128)} %bitcast.3) | data formatting | bytes 98304

commit v3 on v2

--- a/solution.py
+++ b/solution.py
@@ -226,36 +226,47 @@
     part[2] = acc[4]
     mine = pl.ds(pl.multiple_of(c * half, half), half)
     other = pl.ds(pl.multiple_of((1 - c) * half, half), half)
-    first = pltpu.make_async_remote_copy(
-        src_ref=part.at[:, other, :], dst_ref=rx1, send_sem=t_sem.at[0], recv_sem=r_sem.at[0],
-        device_id=(me, mate), device_id_type=MESH,
-    )
-    first.start()
-    first.wait_recv()
-    both = part[:, mine, :] + rx1[...]
-    chip[...] = both
-    sx2[...] = both.astype(BF16)
+    first = [
+        pltpu.make_async_remote_copy(
+            src_ref=part.at[k, other, :], dst_ref=rx1.at[k], send_sem=t_sem.at[0, k],
+            recv_sem=r_sem.at[0, k], device_id=(me, mate), device_id_type=MESH,
+        )
+        for k in range(3)
+    ]
     swaps = [
+        [
+            pltpu.make_async_remote_copy(
+                src_ref=sx2.at[k], dst_ref=rx2.at[j - 1, k], send_sem=t2_sem.at[j - 1, k],
+                recv_sem=r2_sem.at[j - 1, k],
+                device_id=(me, ((y + j) % ny) * 2 + c), device_id_type=MESH,
+            )
+            for j in range(1, ny)
+        ]
+        for k in range(3)
+    ]
+    last = [
         pltpu.make_async_remote_copy(
-            src_ref=sx2, dst_ref=rx2.at[j - 1], send_sem=t2_sem.at[j - 1],
-            recv_sem=r2_sem.at[j - 1],
-            device_id=(me, ((y + j) % ny) * 2 + c), device_id_type=MESH,
-        )
-        for j in range(1, ny)
+            src_ref=full.at[c, k], dst_ref=full.at[c, k], send_sem=t_sem.at[1, k],
+            recv_sem=r_sem.at[1, k], device_id=(me, mate), device_id_type=MESH,
+        )
+        for k in range(3)
     ]
-    for copy in swaps:
+    for copy in first:
         copy.start()
-    for copy in swaps:
-        copy.wait_recv()
-    whole = chip[...]
-    for j in range(1, ny):
-        whole = whole + rx2[j - 1].astype(F32)
-    full[c] = whole
-    last = pltpu.make_async_remote_copy(
-        src_ref=full.at[c], dst_ref=full.at[c], send_sem=t_sem.at[1], recv_sem=r_sem.at[1],
-        device_id=(me, mate), device_id_type=MESH,
-    )
-    last.start()
+    for k in range(3):
+        first[k].wait_recv()
+        both = part[k, mine, :] + rx1[k]
+        chip[k] = both
+        sx2[k] = both.astype(BF16)
+        for copy in swaps[k]:
+            copy.start()
+    for k in range(3):
+        whole = chip[k]
+        for j in range(1, ny):
+            swaps[k][j - 1].wait_recv()
+            whole = whole + rx2[j - 1, k].astype(F32)
+        full[c, k] = whole
+        last[k].start()
 
     start, length, seen = jnp.int32(0), jnp.int32(0), jnp.int32(0)
     for e in range(2 * ny):
@@ -263,7 +274,8 @@
         start = jnp.where(hit, seen, start)
         length = jnp.where(hit, lens[0, e], length)
         seen = seen + lens[0, e]
-    last.wait_recv()
+    for copy in last:
+        copy.wait_recv()
 
     places = lax.broadcasted_iota(jnp.int32, (half, 128), 0)
     pair_one = jnp.zeros((128, 128), F32)
@@ -286,10 +298,11 @@
     odd = fs[pl.ds(1, 96, stride=2), :]
     out[...] = jnp.concatenate([even[:, :64], odd[:, :64]], axis=1)
 
-    first.wait_send()
-    last.wait_send()
-    for copy in swaps:
-        copy.wait_send()
+    for k in range(3):
+        first[k].wait_send()
+        last[k].wait_send()
+        for copy in swaps[k]:
+            copy.wait_send()
 
     def drain(src_z, carry):
         slot = src_z * nx + x
@@ -363,10 +376,10 @@
             dma((ndp, 1 + len(PIECES))),
             dma((ndp, 1 + len(PIECES))),
             dma((ndp, 1 + len(PIECES), nx - 1)),
-            dma((2,)),
-            dma((2,)),
-            dma((ny - 1,)),
-            dma((ny - 1,)),
+            dma((2, 3)),
+            dma((2, 3)),
+            dma((ny - 1, 3)),
+            dma((ny - 1, 3)),
         ],
         compiler_params=pltpu.CompilerParams(
             collective_id=0, has_side_effects=True, vmem_limit_bytes=62 << 20

time: 50.5 us -> 50.4 us (level)
  no operation moved by 1% of the time
where the time goes in v3:
time: 50.4 us; the launch traced here: 50.1 us
  Pallas kernels  48.7 us (97%)
  local copies, waits for them, and re-layouts  1.42 us (3%)
    pallas_call x1, Pallas kernels, fused(): pl.pallas_call(functools.partial(kernel, nz, nx, ny), out_shape=jax.Shape...  48.7 us
    unnamed x1, local copies, waits for them, and re-layouts  1.42 us

profile of v3, /device:TPU:0, one launch (start us, length us, event | category | flops | bytes accessed | tf_op | source)
XLA Modules:
  0.0 50.1 jit_solution(451588729865526741)
XLA Ops:
  0.0 48.7 %shard_map.91 = f32[96,128]{1,0:T(8,128)} custom-call(bf16[256,2048]{1,0:T(8,128)(2,1)} %inp_h.1, bf16[256,2048]{1,0:T(8,128)(2,1)} %og_h.1, bf16[256,7168]{1,0:T(8,128)(2,1)} %gp_h.1, bf16[256,7168]{1,0:T(8,128)(2,1)} %up_h.1, bf16[256,7168]{1,0:T(8,128)(2,1)} %hg_h.1, bf16[256,128]{1,0:T(8,128)(2,1)} %pm_h.1, bf16[192,896]{1,0:T(8,128)(2,1)} %bitcast.2, ...), custom_call_target="tpu_custom_call" | custom-call | tf_op jit(solution)/shard_map/pallas_call | solution.py:352
  48.7 1.4 %copy.11 = f32[1,12288]{1,0:T(1,128)} copy(f32[1,12288]{1,0:T(1,128)} %bitcast.3) | data formatting | bytes 98304
